TPU v7x, 32 devices: a whole 2x2x4 slice. The times are simulated.
32 devices in a mesh: shot: 4 (over z), rcv: 8 (over y, x, core).
Axes of the slice: x: 2, y: 2, z: 4, core: 2. Of those that a mesh axis runs over, the one named last changes fastest.
Arguments:
- traces: bfloat16 [768, 768, 512], P('shot', 'rcv'), may hold values from -6 to 6
- source_weight: float32 [2, 256, 768], P(None, ('shot', 'rcv')), may hold values from -0.15625 to 0.15625
Outputs:
- multiples: bfloat16 [768, 768, 512], P('shot', 'rcv')
All inputs are finite; a program needn't handle non-finite values.
Results may differ from a plain program's by a relative error of at most 0.0092.
Values may be sent and summed in bfloat16 or wider, within the bound.
No kernel may reach another device: no remote copies, remote signals or barrier semaphores. Data moves between devices by JAX's collectives and lax.ppermute only.
A program may use at most 192 MiB of HBM per device.

v0:
```python
import math

import jax
import jax.numpy as jnp
from jax import lax
from jax.sharding import PartitionSpec as P

STATIONS = 768
FREQS = 256


def dft_basis(count_freq, count_time):
    temporal_pitch = jnp.arange(count_freq, dtype=jnp.int32)
    moments = jnp.arange(count_time, dtype=jnp.int32)
    phase = (temporal_pitch[:, None] * moments[None, :] % count_time).astype(jnp.float32) * (
        2.0 * math.pi / count_time
    )
    stacked = jnp.stack([jnp.cos(phase), -jnp.sin(phase)], axis=1)
    return stacked.reshape(2 * count_freq, count_time).astype(jnp.bfloat16)


def predict_single(operands):
    one_slice, one_weight = operands
    summed = one_slice.astype(jnp.float32) + jnp.swapaxes(one_slice, 1, 2).astype(jnp.float32)
    averaged = (0.5 * summed).astype(jnp.bfloat16)
    average_inphase_part = averaged[0]
    average_quadrature_part = averaged[1]
    real_f32 = average_inphase_part.astype(jnp.float32)
    imag_f32 = average_quadrature_part.astype(jnp.float32)
    weight_real = one_weight[0][:, None]
    weight_imag = one_weight[1][:, None]
    emitter_scaled_inphase = (weight_real * real_f32 - weight_imag * imag_f32).astype(jnp.bfloat16)
    emitter_scaled_quadrature = (weight_real * imag_f32 + weight_imag * real_f32).astype(
        jnp.bfloat16
    )
    left_operand = jnp.concatenate([average_inphase_part, average_quadrature_part], axis=1)
    upper = jnp.concatenate([emitter_scaled_inphase, emitter_scaled_quadrature], axis=1)
    lower = jnp.concatenate([-emitter_scaled_quadrature, emitter_scaled_inphase], axis=1)
    second_factor = jnp.concatenate([upper, lower], axis=0)
    complex_product = jnp.dot(left_operand, second_factor, preferred_element_type=jnp.float32)
    order_rows, double_cols = complex_product.shape
    split_parts = complex_product.reshape(order_rows, 2, double_cols // 2)
    return split_parts.transpose(1, 0, 2).astype(jnp.bfloat16)


def predict_slices(slices, weights):
    return lax.map(predict_single, (slices, jnp.swapaxes(weights, 0, 1)))


def on_device(traces, source_weight):
    shot_dev, rcv_dev, samples = traces.shape
    stations = STATIONS
    frequencies = FREQS
    shot_count = lax.axis_size("shot")
    rcv_count = lax.axis_size("rcv")
    traces_local = shot_dev * rcv_dev
    freq_local = frequencies // (shot_count * rcv_count)
    basis = dft_basis(frequencies, samples)
    flattened = traces.reshape(traces_local, samples)
    spectra = lax.dot_general(
        basis, flattened, (((1,), (1,)), ((), ())), preferred_element_type=jnp.float32
    )
    spectra = (
        (spectra * samples ** (-0.5))
        .astype(jnp.bfloat16)
        .reshape(frequencies, 2, shot_dev, rcv_dev)
    )
    received = lax.all_to_all(spectra, ("shot", "rcv"), split_axis=0, concat_axis=3, tiled=True)
    received = received.reshape(freq_local, 2, shot_dev, shot_count, stations)
    slices = received.transpose(0, 1, 3, 2, 4).reshape(freq_local, 2, stations, stations)
    predicted = predict_slices(slices, source_weight)
    outgoing = predicted.reshape(freq_local, 2, shot_count, shot_dev, stations)
    outgoing = outgoing.transpose(0, 1, 3, 2, 4).reshape(
        freq_local, 2, shot_dev, shot_count * stations
    )
    returned = lax.all_to_all(outgoing, ("shot", "rcv"), split_axis=3, concat_axis=0, tiled=True)
    gathered = returned.reshape(2 * frequencies, traces_local)
    series = lax.dot_general(
        gathered, basis, (((0,), (0,)), ((), ())), preferred_element_type=jnp.float32
    )
    series = (series * (2.0 / samples) ** 0.5).astype(jnp.bfloat16)
    return series.reshape(shot_dev, rcv_dev, samples)


def solution(mesh):
    placed = (P("shot", "rcv", None), P(None, ("shot", "rcv"), None))
    return jax.shard_map(
        on_device, mesh=mesh, in_specs=placed, out_specs=P("shot", "rcv", None), check_vma=False
    )
```

profile of v0, /device:TPU:0, one launch (start us, length us, event | category | flops | bytes accessed | tf_op | source)
XLA Modules:
  0.0 1702.9 jit_solution(4522176417831185349)
XLA Ops:
  3.0 21.1 %multiply_convert_fusion.1 = bf16[512,18432]{1,0:T(8,128)(2,1)} fusion(bf16[512,512]{1,0:T(8,128)(2,1)S(1)} %convert_element_type.74, bf16[18432,512]{1,0:T(8,128)(2,1)} %bitcast.78), kind=kOutput, calls=%fused_computation.31 | convolution fusion | flops 9682550784 | bytes 38273024 | tf_op jit(solution)/shard_map/dot_general | solution.py:60
  24.2 36.1 %reshape.120 = bf16[256,2,192,96]{3,2,1,0:T(8,128)(2,1)} reshape(bf16[512,18432]{1,0:T(8,128)(2,1)} %multiply_convert_fusion.1) | data formatting | bytes 37748736 | tf_op jit(solution)/shard_map/reshape | solution.py:66
  60.2 7.4 all-to-all-start
  67.7 561.0 %all-to-all-done = bf16[256,2,192,96]{3,2,1,0:T(8,128)(2,1)} async-done(((bf16[256,2,192,96]{3,2,1,0:T(8,128)(2,1)}), bf16[256,2,192,96]{3,2,1,0:T(8,128)(2,1)}, u32[]{:S(2)}, u32[]{:S(2)}) %all-to-all-start) | async-done | bytes 18874400 | tf_op jit(solution)/shard_map/all_to_all | solution.py:68
  628.7 26.9 %copy.42 = bf16[32,8,2,192,96]{4,0,3,2,1:T(8,128)(2,1)} copy(bf16[32,8,2,192,96]{4,3,2,1,0:T(8,128)(2,1)} %bitcast.8) | data formatting | bytes 37748736 | tf_op jit(solution)/shard_map/all_to_all | solution.py:68
  655.6 44.1 %reshape.121 = bf16[8,2,192,4,768]{4,3,2,1,0:T(4,128)(2,1)} reshape(bf16[8,2,192,32,96]{4,3,2,1,0:T(8,128)(2,1)} %bitcast.70) | data formatting | bytes 37748736 | tf_op jit(solution)/shard_map/reshape | solution.py:69
  699.7 18.2 %copy.33 = bf16[8,2,4,192,768]{4,3,2,1,0:T(8,128)(2,1)} copy(bf16[8,2,4,192,768]{4,2,3,1,0:T(4,128)(2,1)} %bitcast.74) | data formatting | bytes 37748736 | tf_op jit(solution)/shard_map/transpose | solution.py:70
  717.9 227.4 %while.10 = (s32[]{:T(128)}, bf16[8,2,768,768]{3,1,2,0:T(2,128)(2,1)}, bf16[8,2,768,768]{3,2,1,0:T(8,128)(2,1)}, f32[8,2,768]{2,1,0:T(2,128)S(1)}, s32[]{:T(128)}, /*index=5*/s32[]{:T(128)}, s32[]{}) while((s32[]{:T(128)}, bf16[8,2,768,768]{3,1,2,0:T(2,128)(2,1)}, bf16[8,2,768,768]{3,2,1,0:T(8,128)(2,1)}, f32[8,2,768]{2,1,0:T(2,128)S(1)}, ...), condition=%wide.region_1.2_spmd, body=%wide.region_0.1_spmd.sunk | while | flops 3662217216 | bytes 56648296 | solution.py:47
  722.1 6.1 copy.46
  750.5 6.1 copy.46
  761.5 5.3 fusion.44
  779.0 6.1 copy.46
  790.0 5.3 fusion.44
  807.4 6.1 copy.46
  835.8 6.1 copy.46
  864.3 6.1 copy.46
  892.7 6.1 copy.46
  921.1 6.1 copy.46
  945.4 24.9 %copy.43 = bf16[8,2,4,192,768]{4,2,3,1,0:T(4,128)(2,1)} copy(bf16[8,2,4,192,768]{4,1,3,2,0:T(2,128)(2,1)} %bitcast.76) | data formatting | bytes 37748736 | tf_op jit(solution)/shard_map/reshape | solution.py:72
  970.2 66.2 %copy.38 = bf16[8,2,192,4,768]{2,1,0,4,3:T(2,128)(2,1)} copy(bf16[8,2,192,4,768]{4,3,2,1,0:T(4,128)(2,1)} %bitcast.75) | data formatting | bytes 37748736 | tf_op jit(solution)/shard_map/reshape | solution.py:73
  1036.4 547.7 %all_to_all.30 = bf16[8,2,192,3072]{2,1,0,3:T(2,128)(2,1)} all-to-all(bf16[8,2,192,3072]{2,1,0,3:T(2,128)(2,1)} %bitcast.71), channel_id=1, replica_groups=mesh['shot'=4,'rcv'=8] {'shot','rcv'}, dimensions={3} | all-to-all | bytes 37748736 | tf_op jit(solution)/shard_map/all_to_all | solution.py:76
  1584.1 56.7 %copy.37 = bf16[8,2,192,32,96]{4,2,1,0,3:T(8,128)(2,1)} copy(bf16[8,2,192,32,96]{2,1,0,4,3:T(2,128)(2,1)} %bitcast.69) | data formatting | bytes 37748736 | tf_op jit(solution)/shard_map/all_to_all | solution.py:76
  1640.8 41.7 %reshape.125 = bf16[512,18432]{1,0:T(8,128)(2,1)} reshape(bf16[32,8,2,192,96]{4,3,2,1,0:T(8,128)(2,1)} %bitcast.72) | data formatting | bytes 37748736 | tf_op jit(solution)/shard_map/reshape | solution.py:77
  1682.5 20.4 %multiply_convert_fusion = bf16[18432,512]{1,0:T(8,128)(2,1)} fusion(bf16[512,18432]{1,0:T(8,128)(2,1)} %reshape.125, bf16[512,512]{1,0:T(8,128)(2,1)S(1)} %copy-done.1), kind=kOutput, calls=%fused_computation.30 | convolution fusion | flops 9682550784 | bytes 38273024 | tf_op jit(solution)/shard_map/dot_general | solution.py:78
  (82 shorter events, 170.9 us)
Async XLA Ops:
  3.0 21.2 %copy-start = (bf16[512,512]{1,0:T(8,128)(2,1)}, bf16[512,512]{1,0:T(8,128)(2,1)S(1)}, u32[]{:S(2)}) copy-start(bf16[512,512]{1,0:T(8,128)(2,1)S(1)} %convert_element_type.74) | copy-start | bytes 1572868
  60.2 7.5 copy-start.2
  60.2 568.5 %all-to-all-start = ((bf16[256,2,192,96]{3,2,1,0:T(8,128)(2,1)}), bf16[256,2,192,96]{3,2,1,0:T(8,128)(2,1)}, u32[]{:S(2)}, u32[]{:S(2)}) async-start(bf16[256,2,192,96]{3,2,1,0:T(8,128)(2,1)} %reshape.120), calls=%async_computation | async-start | bytes 50331648 | tf_op jit(solution)/shard_map/all_to_all | solution.py:68
  1640.8 41.7 %copy-start.1 = (bf16[512,512]{1,0:T(8,128)(2,1)S(1)}, bf16[512,512]{1,0:T(8,128)(2,1)}, u32[]{:S(2)}) copy-start(bf16[512,512]{1,0:T(8,128)(2,1)} %copy-done) | copy-start | bytes 1572868
where the time goes:
time: 1710 us; the launch traced here: 1700 us
  waiting for transfers between devices  561 us (33%)
  blocking collectives  548 us (32%)
  local copies, waits for them, and re-layouts  430 us (25%)
  matrix products  83.7 us (5%)
  other arithmetic  73.2 us (4%)
    all_to_all x1, waiting for transfers between devices, on_device(): lax.all_to_all(spectra, ('shot', 'rcv'), split_axis=0, concat_axis=3, til...  561 us
    all_to_all x1, blocking collectives, on_device(): lax.all_to_all(outgoing, ('shot', 'rcv'), split_axis=3, concat_axis=0, ti...  548 us
    reshape x1, local copies, waits for them, and re-layouts, on_device(): outgoing.transpose(0, 1, 3, 2, 4)  66.2 us
    all_to_all x1, local copies, waits for them, and re-layouts, on_device(): lax.all_to_all(outgoing, ('shot', 'rcv'), split_axis=3, concat_axis=0, ti...  56.7 us
    convert_element_type x8, local copies, waits for them, and re-layouts, predict_single(): one_slice.astype(jnp.float32)  48.7 us
    reshape x1, local copies, waits for them, and re-layouts, on_device(): received = received.reshape(freq_local, 2, shot_dev, shot_count, stations)  44.1 us
    dot_general x8, matrix products, predict_single(): jnp.dot(left_operand, second_factor, preferred_element_type=jnp.float32)  42.1 us
    reshape x1, local copies, waits for them, and re-layouts, on_device(): gathered = returned.reshape(2 * frequencies, traces_local)  41.7 us
  transfers between devices with their start and end apart: 1, of which 1 were waited for; matrix products, arithmetic and copies ran while one was open for 0% of the time, Pallas kernels for 0%

commit v1 on v0

v1 whole, which is shorter than its diff:
```python
import math

import jax
import jax.numpy as jnp
from jax import lax
from jax.experimental import pallas as pl
from jax.experimental.pallas import tpu as pltpu
from jax.sharding import PartitionSpec as P


def dft_basis(count_freq, count_time):
    temporal_pitch = jnp.arange(count_freq, dtype=jnp.int32)
    moments = jnp.arange(count_time, dtype=jnp.int32)
    phase = (temporal_pitch[:, None] * moments[None, :] % count_time).astype(jnp.float32) * (
        2.0 * math.pi / count_time
    )
    stacked = jnp.stack([jnp.cos(phase), -jnp.sin(phase)], axis=1)
    return stacked.reshape(2 * count_freq, count_time).astype(jnp.bfloat16)


def side_by_side(shot_dev, rcv_dev):
    best = None
    for group in range(1, shot_dev + 1):
        if shot_dev % group or (shot_dev // group) % 16:
            continue
        lanes = group * rcv_dev
        fill = lanes / (-(-lanes // 128) * 128)
        if best is None or fill > best[0]:
            best = (fill, group)
    return best[1]


def frequency_kernel(shot_count, rcv_count, shot_dev, rcv_dev, group):
    n = shot_count * shot_dev
    rows = shot_dev // group
    strip = next(t for t in (256, 128, 96, 64, 48, 32, 16) if n % t == 0)
    tile = 128 if n % 128 == 0 else n

    def body(w_ref, in_ref, out_ref, m_ref, a_ref, s_ref):
        for c in range(2):

            def assemble(z, carry):
                for g in range(group):
                    line = jnp.concatenate(
                        [
                            in_ref[z * rcv_count + j, 0, c, :, g * rcv_dev : (g + 1) * rcv_dev]
                            for j in range(rcv_count)
                        ],
                        axis=1,
                    )
                    at = pl.multiple_of(z * shot_dev + g * rows, 16)
                    m_ref[c, pl.ds(at, rows), :] = line
                return carry

            lax.fori_loop(0, shot_count, assemble, 0)

        def average(i, carry):
            at = pl.multiple_of(i * tile, tile)
            parts = []
            for c in range(2):
                own = m_ref[c, pl.ds(at, tile), :].astype(jnp.float32)
                other = m_ref[c, :, pl.ds(at, tile)].T.astype(jnp.float32)
                mean = (0.5 * (own + other)).astype(jnp.bfloat16)
                a_ref[c, pl.ds(at, tile), :] = mean
                parts.append(mean.astype(jnp.float32))
            real, imag = parts
            wr = w_ref[0, pl.ds(at, tile), 0:1]
            wi = w_ref[0, pl.ds(at, tile), 1:2]
            s_ref[0, pl.ds(at, tile), :] = (wr * real - wi * imag).astype(jnp.bfloat16)
            s_ref[1, pl.ds(at, tile), :] = (wr * imag + wi * real).astype(jnp.bfloat16)
            return carry

        lax.fori_loop(0, n // tile, average, 0)

        def product(i, carry):
            at = pl.multiple_of(i * strip, strip)
            ar = a_ref[0, pl.ds(at, strip), :]
            ai = a_ref[1, pl.ds(at, strip), :]
            dot = lambda x, y: jnp.dot(x, y, preferred_element_type=jnp.float32)
            m_ref[0, pl.ds(at, strip), :] = (dot(ar, s_ref[0]) - dot(ai, s_ref[1])).astype(jnp.bfloat16)
            m_ref[1, pl.ds(at, strip), :] = (dot(ar, s_ref[1]) + dot(ai, s_ref[0])).astype(jnp.bfloat16)
            return carry

        lax.fori_loop(0, n // strip, product, 0)

        for c in range(2):

            def split(z, carry):
                pieces = []
                for g in range(group):
                    at = pl.multiple_of(z * shot_dev + g * rows, 16)
                    pieces.append(m_ref[c, pl.ds(at, rows), :])
                for j in range(rcv_count):
                    out_ref[z * rcv_count + j, 0, c] = jnp.concatenate(
                        [p[:, j * rcv_dev : (j + 1) * rcv_dev] for p in pieces], axis=1
                    )
                return carry

            lax.fori_loop(0, shot_count, split, 0)

    return body


def predict(received, weights, shot_count, rcv_count, shot_dev, rcv_dev, group):
    devices, freqs, _, rows, lanes = received.shape
    n = shot_count * shot_dev
    block = pl.BlockSpec((devices, 1, 2, rows, lanes), lambda f: (0, f, 0, 0, 0))
    return pl.pallas_call(
        frequency_kernel(shot_count, rcv_count, shot_dev, rcv_dev, group),
        grid=(freqs,),
        in_specs=[pl.BlockSpec((1, n, 2), lambda f: (f, 0, 0)), block],
        out_specs=block,
        out_shape=jax.ShapeDtypeStruct(received.shape, jnp.bfloat16),
        scratch_shapes=[pltpu.VMEM((2, n, n), jnp.bfloat16)] * 3,
        name="predict",
    )(weights, received)


def on_device(traces, source_weight):
    shot_dev, rcv_dev, samples = traces.shape
    shot_count = lax.axis_size("shot")
    rcv_count = lax.axis_size("rcv")
    devices = shot_count * rcv_count
    freq_local = source_weight.shape[1]
    frequencies = freq_local * devices
    group = side_by_side(shot_dev, rcv_dev)
    rows, lanes = shot_dev // group, group * rcv_dev
    basis = dft_basis(frequencies, samples)
    flat = traces.reshape(group, rows, rcv_dev, samples).transpose(1, 0, 2, 3)
    flat = flat.reshape(rows * lanes, samples)
    spectra = lax.dot_general(
        basis, flat, (((1,), (1,)), ((), ())), preferred_element_type=jnp.float32
    )
    spectra = (spectra * samples ** (-0.5)).astype(jnp.bfloat16)
    spectra = spectra.reshape(devices, freq_local, 2, rows, lanes)
    received = lax.all_to_all(spectra, ("shot", "rcv"), 0, 0)
    weights = jnp.transpose(source_weight, (1, 2, 0))
    predicted = predict(received, weights, shot_count, rcv_count, shot_dev, rcv_dev, group)
    returned = lax.all_to_all(predicted, ("shot", "rcv"), 0, 0)
    returned = returned.reshape(2 * frequencies, rows * lanes)
    series = lax.dot_general(
        returned, basis, (((0,), (0,)), ((), ())), preferred_element_type=jnp.float32
    )
    series = (series * (2.0 / samples) ** 0.5).astype(jnp.bfloat16)
    series = series.reshape(rows, group, rcv_dev, samples).transpose(1, 0, 2, 3)
    return series.reshape(shot_dev, rcv_dev, samples)


def solution(mesh):
    placed = (P("shot", "rcv", None), P(None, ("shot", "rcv"), None))
    return jax.shard_map(
        on_device, mesh=mesh, in_specs=placed, out_specs=P("shot", "rcv", None), check_vma=False
    )
```

time: 1710 us -> 1020 us (0.60)
  local copies, waits for them, and re-layouts: 430 us -> 66.6 us
  waiting for transfers between devices: 561 us -> 417 us
  blocking collectives: 548 us -> 411 us
  Pallas kernels: 0 us -> 76.5 us
  other arithmetic: 73.2 us -> 2.23 us
  matrix products: 83.7 us -> 41.3 us
    reshape x5 -> x0, local copies, waits for them, and re-layouts: 213 us -> none  [the longest x1 66.2 us: on_device(): outgoing.transpose(0, 1, 3, 2, 4)]
    all_to_all x1, waiting for transfers between devices: 561 us -> 417 us  [on_device(): received = lax.all_to_all(spectra, ('shot', 'rcv'), 0, 0)]
    all_to_all x1, blocking collectives: 548 us -> 411 us  [on_device(): returned = lax.all_to_all(predicted, ('shot', 'rcv'), 0, 0)]
    convert_element_type x16 -> x0, local copies, waits for them, and re-layouts: 88.4 us -> none  [the longest x8 48.7 us: predict_single(): one_slice.astype(jnp.float32)]
    all_to_all x2 -> x0, local copies, waits for them, and re-layouts: 83.6 us -> none  [the longest x1 56.7 us: on_device(): lax.all_to_all(outgoing, ('shot', 'rcv'), split_axis=3, concat_axis=0, ti...]
    pallas_call x0 -> x1, Pallas kernels: none -> 76.5 us  [predict(): pl.pallas_call(frequency_kernel(shot_count, rcv_count, shot_dev, rcv_dev,...]
    convert_element_type x24 -> x0, other arithmetic: 66.5 us -> none  [the longest x8 33.5 us: predict_single(): one_slice.astype(jnp.float32)]
    dot_general x10 -> x2, matrix products: 83.7 us -> 41.3 us  [the longest x1 20.9 us: on_device(): lax.dot_general(basis, flat, (((1,), (1,)), ((), ())), preferred_element_...]
where the time goes in v1:
time: 1020 us
  waiting for transfers between devices  417 us (41%)
  blocking collectives  411 us (40%)
  Pallas kernels  76.5 us (8%)
  local copies, waits for them, and re-layouts  66.6 us (7%)
  matrix products  41.3 us (4%)
    all_to_all x1, waiting for transfers between devices, on_device(): received = lax.all_to_all(spectra, ('shot', 'rcv'), 0, 0)  417 us
    all_to_all x1, blocking collectives, on_device(): returned = lax.all_to_all(predicted, ('shot', 'rcv'), 0, 0)  411 us
    pallas_call x1, Pallas kernels, predict(): pl.pallas_call(frequency_kernel(shot_count, rcv_count, shot_dev, rcv_dev,...  76.5 us
    unnamed x5, local copies, waits for them, and re-layouts  31.9 us
    dot_general x1, matrix products, on_device(): lax.dot_general(basis, flat, (((1,), (1,)), ((), ())), preferred_element_...  20.9 us
  transfers between devices with their start and end apart: 1, of which 1 were waited for; matrix products, arithmetic and copies ran while one was open for 0% of the time, Pallas kernels for 0%

profile of v1, /device:TPU:0, one launch (start us, length us, event | category | flops | bytes accessed | tf_op | source)
XLA Modules:
  0.0 1022.5 jit_solution(11528430455562237601)
XLA Ops:
  0.0 2.2 negate_convert_fusion
  2.2 0.1 pad_maximum_fusion
  2.2 0.5 copy.14
  2.8 0.2 convert_element_type.37
  3.0 17.0 %copy.15 = bf16[48,4,96,512]{3,2,1,0:T(8,128)(2,1)} copy(bf16[48,4,96,512]{3,2,0,1:T(8,128)(2,1)} %bitcast.21) | data formatting | bytes 37748736 | tf_op jit(solution)/shard_map/transpose | solution.py:129
  20.0 20.9 %multiply_convert_fusion.1 = bf16[512,18432]{1,0:T(8,128)(2,1)} fusion(bf16[512,512]{1,0:T(8,128)(2,1)S(1)} %convert_element_type.37, bf16[18432,512]{1,0:T(8,128)(2,1)} %bitcast.25), kind=kOutput, calls=%fused_computation.1 | convolution fusion | flops 9682550784 | bytes 38273024 | tf_op jit(solution)/shard_map/dot_general | solution.py:131
  40.9 18.2 %copy.17 = bf16[64,8,48,384]{3,2,1,0:T(8,128)(2,1)} copy(bf16[64,8,48,384]{3,1,2,0:T(8,128)(2,1)} %bitcast.24) | data formatting | bytes 37748736
  59.1 0.0 copy-start
  59.1 7.4 all-to-all-start
  66.5 0.0 copy-done
  66.6 2.2 copy.13
  68.8 417.3 %all-to-all-done.in_ref = bf16[32,8,2,48,384]{4,3,2,1,0:T(8,128)(2,1)} async-done(((bf16[32,8,2,48,384]{4,3,2,1,0:T(8,128)(2,1)}), bf16[32,8,2,48,384]{4,3,2,1,0:T(8,128)(2,1)}, u32[]{:S(2)}, u32[]{:S(2)}) %all-to-all-start) | async-done | bytes 18874400 | tf_op jit(solution)/shard_map/all_to_all | solution.py:136
  486.0 76.5 %predict.1 = bf16[32,8,2,48,384]{4,3,2,1,0:T(8,128)(2,1)} custom-call(f32[8,768,2]{2,1,0:T(8,128)} %bitcast.26, bf16[32,8,2,48,384]{4,3,2,1,0:T(8,128)(2,1)} %all-to-all-done.in_ref), custom_call_target="tpu_custom_call" | custom-call | tf_op jit(solution)/shard_map/predict/pallas_call | solution.py:108
  562.5 411.1 %all_to_all.10 = bf16[32,8,2,48,384]{4,3,2,1,0:T(8,128)(2,1)S(1)} all-to-all(bf16[32,8,2,48,384]{4,3,2,1,0:T(8,128)(2,1)} %predict.1), channel_id=1, replica_groups=mesh['shot'=4,'rcv'=8] {'shot','rcv'}, dimensions={0} | all-to-all | bytes 37748736 | tf_op jit(solution)/shard_map/all_to_all | solution.py:139
  973.7 11.5 %copy.18 = bf16[64,8,48,384]{3,1,2,0:T(8,128)(2,1)} copy(bf16[64,8,48,384]{3,2,1,0:T(8,128)(2,1)S(1)} %bitcast.20) | data formatting | bytes 37748736
  985.2 20.4 %multiply_convert_fusion = bf16[18432,512]{1,0:T(8,128)(2,1)} fusion(bf16[512,18432]{1,0:T(8,128)(2,1)} %bitcast.22, bf16[512,512]{1,0:T(8,128)(2,1)S(1)} %convert_element_type.37), kind=kOutput, calls=%fused_computation | convolution fusion | flops 9682550784 | bytes 38273024 | tf_op jit(solution)/shard_map/dot_general | solution.py:141
  1005.5 17.0 %copy.16 = bf16[4,48,96,512]{3,2,1,0:T(8,128)(2,1)} copy(bf16[4,48,96,512]{3,2,0,1:T(8,128)(2,1)} %bitcast.23) | data formatting | bytes 37748736 | tf_op jit(solution)/shard_map/transpose | solution.py:145
Async XLA Ops:
  59.1 7.5 copy-start
  59.1 426.9 %all-to-all-start = ((bf16[32,8,2,48,384]{4,3,2,1,0:T(8,128)(2,1)}), bf16[32,8,2,48,384]{4,3,2,1,0:T(8,128)(2,1)}, u32[]{:S(2)}, u32[]{:S(2)}) async-start(bf16[32,8,2,48,384]{4,3,2,1,0:T(8,128)(2,1)} %bitcast.19), calls=%async_computation | async-start | bytes 37748736 | tf_op jit(solution)/shard_map/all_to_all | solution.py:136

commit v2 on v1

v2 whole, which is shorter than its diff:
```python
import math

import jax
import jax.numpy as jnp
from jax import lax
from jax.experimental import pallas as pl
from jax.experimental.pallas import tpu as pltpu
from jax.sharding import PartitionSpec as P


def dft_basis(count_freq, count_time):
    temporal_pitch = jnp.arange(count_freq, dtype=jnp.int32)
    moments = jnp.arange(count_time, dtype=jnp.int32)
    phase = (temporal_pitch[:, None] * moments[None, :] % count_time).astype(jnp.float32) * (
        2.0 * math.pi / count_time
    )
    stacked = jnp.stack([jnp.cos(phase), -jnp.sin(phase)], axis=1)
    return stacked.reshape(2 * count_freq, count_time).astype(jnp.bfloat16)


def side_by_side(shot_dev, rcv_dev):
    best = None
    for group in range(1, shot_dev + 1):
        if shot_dev % group or (shot_dev // group) % 16:
            continue
        lanes = group * rcv_dev
        fill = lanes / (-(-lanes // 128) * 128)
        if best is None or fill > best[0]:
            best = (fill, group)
    return best[1]


class Line:
    def __init__(self, size):
        self.size = size
        self.sides = (1, -1)
        self.shifts = [(s, d) for d in range(1, size) for s in self.sides]
        self.tasks = [
            (s, a, e) for a in range(1, size) for e in range(1, size - a) for s in self.sides
        ]

    def inside(self, *places):
        good = True
        for place in places:
            good = good & (place >= 0) & (place < self.size)
        return good

    def clamp(self, place):
        return jnp.clip(place, 0, self.size - 1)

    def count(self, d):
        return self.size - d + 1

    def block(self, n, low, d):
        return jnp.where(n <= low, n, n + d - 1)

    def number(self, block, low, d):
        return jnp.where(block <= low, block, block - d + 1)

    def perm(self, step):
        return [(i, i + step) for i in range(self.size) if 0 <= i + step < self.size]


def matrix_of(ref, at, c, halves, group, rcv_dev):
    lines = [
        jnp.concatenate(
            [ref[at, h, 0, c, :, g * rcv_dev : (g + 1) * rcv_dev] for h in range(halves)], axis=1
        )
        for g in range(group)
    ]
    return jnp.concatenate(lines, axis=0)


def put_matrix(ref, at, c, value, halves, group, rcv_dev, rows):
    for h in range(halves):
        ref[at, h, 0, c] = jnp.concatenate(
            [
                value[g * rows : (g + 1) * rows, h * rcv_dev : (h + 1) * rcv_dev]
                for g in range(group)
            ],
            axis=1,
        )


TOKEN_SPEC = pl.BlockSpec(memory_space=pltpu.SMEM)
TOKEN_SHAPE = jax.ShapeDtypeStruct((1,), jnp.int32)


def in_order(body, grid, in_specs, out_specs, out_shape, scratch=()):
    def whole(pos_ref, *refs):
        token = refs[len(in_specs) + len(out_specs)]
        token[0] = pos_ref[0]
        rest = refs[: len(in_specs) + len(out_specs)] + refs[len(in_specs) + len(out_specs) + 1 :]
        body(pos_ref[0], *rest)

    return pl.pallas_call(
        whole,
        grid_spec=pltpu.PrefetchScalarGridSpec(
            num_scalar_prefetch=1,
            grid=grid,
            in_specs=in_specs,
            out_specs=[*out_specs, TOKEN_SPEC],
            scratch_shapes=list(scratch),
        ),
        out_shape=[*(jax.ShapeDtypeStruct(s, jnp.bfloat16) for s in out_shape), TOKEN_SHAPE],
    )


def step_rows(rows):
    return 16 if rows % 16 == 0 else rows


def transform(place, basis, traces, shape, scale):
    group, rows, rcv_dev, samples = traces.shape
    lanes = group * rcv_dev
    count = basis.shape[0]
    step = step_rows(rows)

    def body(pos, basis_ref, in_ref, out_ref, acc_ref):
        def one(i, carry):
            x = jnp.concatenate([in_ref[g, i] for g in range(group)], axis=0)
            acc_ref[i] = lax.dot_general(
                basis_ref[...], x, (((1,), (1,)), ((), ())), preferred_element_type=jnp.float32
            )
            return carry

        lax.fori_loop(0, step, one, 0, unroll=4)

        def turn(i, carry):
            at = pl.multiple_of(i * 8, 8)
            value = (acc_ref[:, pl.ds(at, 8), :] * scale).swapaxes(0, 1)
            out_ref[pl.ds(at, 8)] = value.astype(jnp.bfloat16)
            return carry

        lax.fori_loop(0, count // 8, turn, 0, unroll=2)

    call = in_order(
        body,
        (rows // step,),
        [
            pl.BlockSpec((count, samples), lambda i, p: (0, 0)),
            pl.BlockSpec((group, step, rcv_dev, samples), lambda i, p: (0, i, 0, 0)),
        ],
        [pl.BlockSpec((count, step, lanes), lambda i, p: (0, i, 0))],
        [(count, rows, lanes)],
        [pltpu.VMEM((step, count, lanes), jnp.float32)],
    )
    out, place = call(place, basis, traces)
    return out.reshape(*shape, rows, lanes), place


def invert(place, basis, parts, group, rcv_dev, scale):
    total, samples = basis.shape
    _, rows, lanes = parts[0].shape
    step = step_rows(rows)

    def body(pos, basis_ref, *refs):
        ins, out_ref, acc_ref = refs[: len(parts)], refs[len(parts)], refs[len(parts) + 1]
        start = 0
        for part, ref in zip(parts, ins):

            def turn(i, carry, ref=ref, start=start):
                at = pl.multiple_of(i * 16, 16)
                value = ref[pl.ds(at, 16)].astype(jnp.float32).swapaxes(0, 1)
                acc_ref[:, pl.ds(start + at, 16), :] = value.astype(jnp.bfloat16)
                return carry

            lax.fori_loop(0, part.shape[0] // 16, turn, 0, unroll=2)
            start += part.shape[0]

        def one(i, carry):
            value = lax.dot_general(
                acc_ref[i], basis_ref[...], (((0,), (0,)), ((), ())),
                preferred_element_type=jnp.float32,
            )
            value = (value * scale).astype(jnp.bfloat16)
            for g in range(group):
                out_ref[g, i] = value[g * rcv_dev : (g + 1) * rcv_dev]
            return carry

        lax.fori_loop(0, step, one, 0, unroll=4)

    call = in_order(
        body,
        (rows // step,),
        [pl.BlockSpec((total, samples), lambda i, p: (0, 0))]
        + [pl.BlockSpec((x.shape[0], step, lanes), lambda i, p: (0, i, 0)) for x in parts],
        [pl.BlockSpec((group, step, rcv_dev, samples), lambda i, p: (0, i, 0, 0))],
        [(group, rows, rcv_dev, samples)],
        [pltpu.VMEM((step, total, lanes), jnp.bfloat16)],
    )
    return call(place, basis, *parts)


def first_sends(line, here, table):
    _, halves, _, freqs, _, rows, lanes = table.shape
    received = []
    for s, a, e in line.tasks:
        j, q = line.clamp(here + s * a), line.clamp(here + s * (a + e))
        piece = lax.dynamic_slice(
            table, (j, 0, q, 0, 0, 0, 0), (1, halves, 1, freqs, 2, rows, lanes)
        )
        piece = piece.reshape(1, halves, freqs, 2, rows, lanes)
        received.append(lax.ppermute(piece, "shot", line.perm(s * a)))
    return received


def pack(place, line, table, received, group, rcv_dev):
    size, halves, _, freqs, _, rows, lanes = table.shape
    unit = (halves, 1, 2, rows, lanes)

    def body(z, *refs):
        own, rest = refs[: len(line.shifts)], refs[len(line.shifts) :]
        other, out = rest[: len(line.tasks)], rest[len(line.tasks) :]
        for m, (s, d) in enumerate(line.shifts):
            q = z + s * d
            low = jnp.minimum(z, q)
            for n in range(line.count(d)):
                block = line.block(n, low, d)

                @pl.when(line.inside(q) & (s * (block - z) >= 0))
                def _(m=m, n=n, block=block):
                    out[m][n] = own[m][line.clamp(block)]

        for t, (s, a, e) in enumerate(line.tasks):
            m = line.shifts.index((s, e))
            block, q = z - s * a, z + s * e

            @pl.when(line.inside(block, q))
            def _(t=t, m=m, block=block, q=q, e=e):
                n = jnp.clip(line.number(block, jnp.minimum(z, q), e), 0, line.count(e) - 1)
                for c in range(2):
                    mine = matrix_of(own[m], line.clamp(block), c, halves, group, rcv_dev)
                    theirs = matrix_of(other[t], 0, c, halves, group, rcv_dev)
                    mean = 0.5 * (mine.astype(jnp.float32) + theirs.T.astype(jnp.float32))
                    put_matrix(out[m], n, c, mean.astype(jnp.bfloat16), halves, group, rcv_dev, rows)

    def own_spec(s, d):
        return pl.BlockSpec(
            (size, halves, None, 1, 2, rows, lanes),
            lambda f, p: (0, 0, line.clamp(p[0] + s * d), f, 0, 0, 0),
        )

    def flat(count):
        return pl.BlockSpec((count,) + unit, lambda f, p: (0, 0, f, 0, 0, 0))

    counts = [line.count(d) for s, d in line.shifts]
    call = in_order(
        body,
        (freqs,),
        [own_spec(*x) for x in line.shifts] + [flat(1)] * len(line.tasks),
        [flat(x) for x in counts],
        [(x, halves, freqs, 2, rows, lanes) for x in counts],
    )
    *messages, place = call(place, *([table] * len(line.shifts)), *received)
    return messages, place


def predict(place, line, table, messages, weights, group, rcv_dev, straight_out):
    straight_in = messages is None
    messages = messages or []
    size = line.size
    halves = table.shape[0] // size if straight_in else table.shape[1]
    freqs, _, rows, lanes = table.shape[-4:]
    shot_dev = group * rows
    rcv_count = size * halves
    n_all = size * shot_dev
    unit = (halves, 1, 2, rows, lanes)
    strip = next(t for t in (256, 128, 96, 64, 48, 32, 16) if n_all % t == 0)
    tile = 128 if n_all % 128 == 0 else n_all
    shifts = line.shifts

    def body(owner, w_ref, own_ref, *refs):
        ins, outs = refs[: len(messages)], refs[len(messages) : -4]
        v_ref, m_ref, a_ref, s_ref = refs[-4:]

        def placed(ref, straight, z, j, m):
            if straight:
                return ref.at[j, lax.rem(m + size, size), 0]
            return v_ref.at[z, j // halves, j % halves, 0]

        def each_block(act):
            for m, (s, d) in enumerate(shifts):
                z = owner - s * d
                low = jnp.minimum(z, owner)

                @pl.when(line.inside(z))
                def _(m=m, d=d, z=z, low=low):
                    for n in range(line.count(d)):
                        act(m, n, line.clamp(z), line.clamp(line.block(n, low, d)))

        def take(m, n, z, block):
            v_ref[z, block] = ins[m][n]

        if not straight_in:
            v_ref[owner] = own_ref[...]
            each_block(take)
        for c in range(2):

            def assemble(z, carry):
                for g in range(group):
                    cut = slice(g * rcv_dev, (g + 1) * rcv_dev)
                    m_ref[c, pl.ds(pl.multiple_of(z * shot_dev + g * rows, 16), rows), :] = (
                        jnp.concatenate(
                            [
                                placed(own_ref, straight_in, z, j, owner - z)[c, :, cut]
                                for j in range(rcv_count)
                            ],
                            axis=1,
                        )
                    )
                return carry

            lax.fori_loop(0, size, assemble, 0)

        def block_of(index):
            return sum((index >= i * shot_dev).astype(jnp.int32) for i in range(1, size))

        def average(i, carry):
            at = pl.multiple_of(i * tile, tile)
            row = block_of(lax.broadcasted_iota(jnp.int32, (tile, n_all), 0) + at)
            col = block_of(lax.broadcasted_iota(jnp.int32, (tile, n_all), 1))
            behind = (owner > row) & (owner > col)
            ahead = (owner < row) & (owner < col)
            keep_own = (behind & (row > col)) | (ahead & (row < col))
            keep_other = (behind & (row < col)) | (ahead & (row > col))
            parts = []
            for c in range(2):
                own = m_ref[c, pl.ds(at, tile), :].astype(jnp.float32)
                other = m_ref[c, :, pl.ds(at, tile)].T.astype(jnp.float32)
                mean = 0.5 * (own + other)
                if not straight_in:
                    mean = jnp.where(keep_own, own, jnp.where(keep_other, other, mean))
                mean = mean.astype(jnp.bfloat16)
                a_ref[c, pl.ds(at, tile), :] = mean
                parts.append(mean.astype(jnp.float32))
            real, imag = parts
            wr = w_ref[0, pl.ds(at, tile), 0:1]
            wi = w_ref[0, pl.ds(at, tile), 1:2]
            s_ref[0, pl.ds(at, tile), :] = (wr * real - wi * imag).astype(jnp.bfloat16)
            s_ref[1, pl.ds(at, tile), :] = (wr * imag + wi * real).astype(jnp.bfloat16)
            return carry

        lax.fori_loop(0, n_all // tile, average, 0)

        def product(i, carry):
            at = pl.multiple_of(i * strip, strip)
            ar = a_ref[0, pl.ds(at, strip), :]
            ai = a_ref[1, pl.ds(at, strip), :]
            dot = lambda x, y: jnp.dot(x, y, preferred_element_type=jnp.float32)
            real = dot(ar, s_ref[0]) - dot(ai, s_ref[1])
            imag = dot(ar, s_ref[1]) + dot(ai, s_ref[0])
            m_ref[0, pl.ds(at, strip), :] = real.astype(jnp.bfloat16)
            m_ref[1, pl.ds(at, strip), :] = imag.astype(jnp.bfloat16)
            return carry

        lax.fori_loop(0, n_all // strip, product, 0)
        for c in range(2):

            def split(z, carry):
                pieces = []
                for g in range(group):
                    at = pl.multiple_of(z * shot_dev + g * rows, 16)
                    pieces.append(m_ref[c, pl.ds(at, rows), :])
                for j in range(rcv_count):
                    v_ref[z, j // halves, j % halves, 0, c] = jnp.concatenate(
                        [p[:, j * rcv_dev : (j + 1) * rcv_dev] for p in pieces], axis=1
                    )
                return carry

            lax.fori_loop(0, size, split, 0)

        def give(m, n, z, block):
            outs[1 + m][n] = v_ref[z, block]

        if straight_out:

            def move(z, carry):
                for j in range(rcv_count):
                    outs[0][j, lax.rem(z - owner + size, size)] = v_ref[z, j // halves, j % halves]
                return carry

            lax.fori_loop(0, size, move, 0)
        else:
            outs[0][...] = v_ref[owner]
            each_block(give)

    def flat(count):
        return pl.BlockSpec((count,) + unit, lambda f, p: (0, 0, f, 0, 0, 0))

    counts = [line.count(d) for s, d in shifts]
    square = pltpu.VMEM((2, n_all, n_all), jnp.bfloat16)
    whole = pl.BlockSpec(
        (rcv_count, size, 1, 2, rows, lanes), lambda f, p: (0, 0, f, 0, 0, 0)
    )
    own_rows = pl.BlockSpec(
        (size, halves, None, 1, 2, rows, lanes), lambda f, p: (0, 0, p[0], f, 0, 0, 0)
    )
    firsts = [size, *counts]
    call = in_order(
        body,
        (freqs,),
        [
            pl.BlockSpec((1, n_all, 2), lambda f, p: (f, 0, 0)),
            whole if straight_in else own_rows,
        ]
        + [flat(x.shape[0]) for x in messages],
        [whole] if straight_out else [flat(x) for x in firsts],
        [(rcv_count, size, freqs, 2, rows, lanes)]
        if straight_out
        else [(x, halves, freqs, 2, rows, lanes) for x in firsts],
        [pltpu.VMEM((size, size) + unit, jnp.bfloat16), square, square, square],
    )
    *outs, place = call(place, weights, table, *messages)
    return outs[0] if straight_out else outs, place


def turn(place, line, messages, group, rcv_dev):
    _, halves, freqs, _, rows, lanes = messages[0].shape
    tasks = line.tasks

    def body(j, *refs):
        own, out = refs[: len(tasks)], refs[len(tasks) :]
        for t, (s, a, e) in enumerate(tasks):

            @pl.when(line.inside(j - s * a, j + s * e))
            def _(t=t):
                for c in range(2):
                    value = matrix_of(own[t], 0, c, halves, group, rcv_dev)
                    put_matrix(out[t], 0, c, value.T, halves, group, rcv_dev, rows)

    def spec(s, a, e):
        def index(f, p):
            j = p[0]
            n = line.number(line.clamp(j - s * a), jnp.minimum(j, j + s * e), e)
            return (jnp.clip(n, 0, line.count(e) - 1), 0, f, 0, 0, 0)

        return pl.BlockSpec((1, halves, 1, 2, rows, lanes), index)

    flat = pl.BlockSpec((1, halves, 1, 2, rows, lanes), lambda f, p: (0, 0, f, 0, 0, 0))
    by_shift = dict(zip(line.shifts, messages))
    call = in_order(
        body,
        (freqs,),
        [spec(*t) for t in tasks],
        [flat] * len(tasks),
        [(1, halves, freqs, 2, rows, lanes)] * len(tasks),
    )
    *turned, place = call(place, *[by_shift[(s, e)] for s, a, e in tasks])
    return turned, place


def unpack(place, line, own, messages, turned):
    size, halves, freqs, _, rows, lanes = own.shape
    unit = (halves, 1, 2, rows, lanes)

    def body(z, own_ref, *refs):
        ins, rest = refs[: len(line.shifts)], refs[len(line.shifts) :]
        late, out = rest[: len(line.tasks)], rest[len(line.tasks)]
        out[:, :, z] = own_ref[...]
        for m, (s, d) in enumerate(line.shifts):
            q = z + s * d
            low = jnp.minimum(z, q)

            @pl.when(line.inside(q))
            def _(m=m, d=d, q=q, low=low):
                for n in range(line.count(d)):
                    out[line.clamp(line.block(n, low, d)), :, line.clamp(q)] = ins[m][n]

        for t, (s, a, e) in enumerate(line.tasks):
            block, q = z + s * a, z + s * (a + e)

            @pl.when(line.inside(q))
            def _(t=t, block=block, q=q):
                out[line.clamp(block), :, line.clamp(q)] = late[t][0]

    def flat(count):
        return pl.BlockSpec((count,) + unit, lambda f, p: (0, 0, f, 0, 0, 0))

    call = in_order(
        body,
        (freqs,),
        [flat(size)] + [flat(line.count(d)) for s, d in line.shifts] + [flat(1)] * len(line.tasks),
        [pl.BlockSpec((size, halves, size, 1, 2, rows, lanes), lambda f, p: (0, 0, 0, f, 0, 0, 0))],
        [(size, halves, size, freqs, 2, rows, lanes)],
    )
    return call(place, own, *messages, *turned)


def chunk_sizes(count):
    if count % 4 == 0:
        return [count // 4, count // 2, count // 4]
    if count % 2 == 0:
        return [count // 2] * 2
    return [count]


def running_order(chunks):
    orders = {
        1: ["D0 X0 M0", "Y0 B0"],
        2: ["D0 D1 X1 S1", "P1 X0 M1 M0", "Y1 T0 B1 U0", "Y0"],
        3: [
            "D1 X1 D0 D2",
            "S1 X2 P1 S2",
            "X0 M0 P2 M1",
            "T0 M2 Y2 U0",
            "Y0 T1 U1 Y1",
            "B2",
        ],
    }
    return [(x[0], int(x[1])) for part in orders[chunks] for x in part.split()]


def pipeline(traces, source_weight):
    shot_dev, rcv_dev, samples = traces.shape
    shot_count = lax.axis_size("shot")
    rcv_count = lax.axis_size("rcv")
    devices = shot_count * rcv_count
    freq_local = source_weight.shape[1]
    frequencies = freq_local * devices
    group = side_by_side(shot_dev, rcv_dev)
    rows, lanes = shot_dev // group, group * rcv_dev
    halves = rcv_count // shot_count
    line = Line(shot_count)
    here = lax.axis_index("shot").astype(jnp.int32)
    place = here.reshape(1)
    sizes = chunk_sizes(freq_local)
    chunks = len(sizes)
    plain = chunks - 1
    cuts = [slice(sum(sizes[:k]), sum(sizes[: k + 1])) for k in range(chunks)]
    basis = dft_basis(frequencies, samples)
    table = basis.reshape(shot_count, rcv_count, freq_local, 2, samples)
    straight = table[:, :, cuts[0]].reshape(-1, samples)
    ending = table[:, :, cuts[plain]].reshape(shot_count, -1, samples)
    table = table.swapaxes(0, 1)
    basis = [table[:, :, cut].reshape(-1, samples) for cut in cuts]
    traces = traces.reshape(group, rows, rcv_dev, samples)
    weights = jnp.transpose(source_weight, (1, 2, 0))
    spectra, tables, early, sent, owned, back, late, final, done = ({} for _ in range(9))

    def around(piece, m):
        if m == 0:
            return piece
        return lax.ppermute(
            piece, "shot", [(i, (i + m) % shot_count) for i in range(shot_count)]
        )

    def shift_along(messages, sign):
        return [
            lax.ppermute(x, "shot", line.perm(sign * s * d))
            for x, (s, d) in zip(messages, line.shifts)
        ]

    for kind, k in running_order(chunks):
        each = sizes[k]
        if kind == "D":
            shape = (rcv_count, shot_count) if k else (shot_count, rcv_count)
            spectra[k], place = transform(
                place, basis[k] if k else straight, traces, shape + (each, 2),
                samples ** (-0.5),
            )
            if not k:
                spectra[k] = [
                    lax.dynamic_index_in_dim(spectra[k], (here + m) % shot_count, 0, False)
                    for m in range(shot_count)
                ]
                spectra[k] = [around(x, m) for m, x in enumerate(spectra[k])]
        elif kind == "X":
            if k:
                table = lax.all_to_all(spectra[k], "rcv", 0, 0)
                tables[k] = table.reshape(
                    shot_count, halves, shot_count, each, 2, rows, lanes
                )
            else:
                tables[k] = lax.all_to_all(jnp.stack(spectra[k], axis=1), "rcv", 0, 0)
        elif kind == "S":
            early[k] = first_sends(line, here, tables[k])
        elif kind == "P":
            messages, place = pack(place, line, tables[k], early[k], group, rcv_dev)
            sent[k] = shift_along(messages, 1)
        elif kind == "M":
            part = weights[cuts[k]]
            last = k == plain
            out, place = predict(place, line, tables[k], sent.get(k), part, group, rcv_dev, last)
            if last:
                final[k] = out
            else:
                owned[k] = out[0]
                back[k] = shift_along(out[1:], -1)
        elif kind == "T":
            turned, place = turn(place, line, back[k], group, rcv_dev)
            late[k] = [
                lax.ppermute(x, "shot", line.perm(-s * a))
                for x, (s, a, e) in zip(turned, line.tasks)
            ]
        elif kind == "U":
            out, place = unpack(place, line, owned[k], back[k], late[k])
            final[k] = out.reshape(rcv_count, shot_count, each, 2, rows, lanes)
        elif kind == "Y":
            done[k] = lax.all_to_all(final[k], "rcv", 0, 0)
        elif kind == "B":
            tail = [around(done[k][:, m], m) for m in range(shot_count)]
    others = [k for k in range(chunks) if k != plain]
    parts = [done[k].reshape(-1, rows, lanes) for k in others]
    parts += [x.reshape(-1, rows, lanes) for x in tail]
    orders = [basis[k] for k in others]
    orders += [
        lax.dynamic_index_in_dim(ending, (here - m) % shot_count, 0, False)
        for m in range(shot_count)
    ]
    series, place = invert(
        place, jnp.concatenate(orders, axis=0), parts, group, rcv_dev, (2.0 / samples) ** 0.5,
    )
    return series.reshape(shot_dev, rcv_dev, samples)


def solution(mesh):
    placed = (P("shot", "rcv", None), P(None, ("shot", "rcv"), None))
    return jax.shard_map(
        pipeline, mesh=mesh, in_specs=placed, out_specs=P("shot", "rcv", None), check_vma=False
    )
```

time: 1020 us -> 1190 us (1.17)
  blocking collectives: 411 us -> 60 us
  starting transfers between devices: 7.44 us -> 299 us
  waiting for transfers between devices: 417 us -> 574 us
  Pallas kernels: 76.5 us -> 222 us
  local copies, waits for them, and re-layouts: 66.6 us -> 24.9 us
  matrix products: 41.3 us -> 0 us
    ppermute x0 -> x54, waiting for transfers between devices: none -> 571 us  [the longest x24 284 us: shift_along(): lax.ppermute(x, 'shot', line.perm(sign * s * d))]
    all_to_all x1 -> x5, waiting for transfers between devices: 417 us -> 2.66 us  [the longest x3 2.65 us: pipeline(): done[k] = lax.all_to_all(final[k], 'rcv', 0, 0)]
    all_to_all x1, blocking collectives: 411 us -> 60 us  [pipeline(): table = lax.all_to_all(spectra[k], 'rcv', 0, 0)]
    ppermute x0 -> x54, starting transfers between devices: none -> 275 us  [the longest x24 120 us: shift_along(): lax.ppermute(x, 'shot', line.perm(sign * s * d))]
    pallas_call x1 -> x13, Pallas kernels: 76.5 us -> 222 us  [the longest x3 107 us: predict(): *outs, place = call(place, weights, table, *messages)]
    dot_general x2 -> x0, matrix products: 41.3 us -> none  [the longest x1 20.9 us: on_device(): lax.dot_general(basis, flat, (((1,), (1,)), ((), ())), preferred_element_...]
    transpose x2 -> x0, local copies, waits for them, and re-layouts: 33.9 us -> none  [the longest x1 17 us: on_device(): flat = traces.reshape(group, rows, rcv_dev, samples).transpose(1, 0, 2, 3)]
    unnamed x5 -> x70, local copies, waits for them, and re-layouts: 31.9 us -> 5.72 us
  transfers between devices with their start and end apart: 1 -> 59, of which waited for: 1 -> 23; matrix products, arithmetic and copies ran while one was open for 0% -> 2% of each run, Pallas kernels for 0% -> 9%
where the time goes in v2:
time: 1190 us
  waiting for transfers between devices  574 us (48%)
  starting transfers between devices  299 us (25%)
  Pallas kernels  222 us (19%)
  blocking collectives  60 us (5%)
  local copies, waits for them, and re-layouts  24.9 us (2%)
    ppermute x24, waiting for transfers between devices, shift_along(): lax.ppermute(x, 'shot', line.perm(sign * s * d))  284 us
    ppermute x6, waiting for transfers between devices, around(): lax.ppermute(piece, 'shot', [(i, (i + m) % shot_count) for i in range(sho...  200 us
    ppermute x24, starting transfers between devices, shift_along(): lax.ppermute(x, 'shot', line.perm(sign * s * d))  120 us
    pallas_call x3, Pallas kernels, predict(): *outs, place = call(place, weights, table, *messages)  107 us
    ppermute x12, starting transfers between devices, pipeline(): lax.ppermute(x, 'shot', line.perm(-s * a))  100 us
    all_to_all x1, blocking collectives, pipeline(): table = lax.all_to_all(spectra[k], 'rcv', 0, 0)  60 us
    ppermute x12, waiting for transfers between devices, pipeline(): lax.ppermute(x, 'shot', line.perm(-s * a))  58.5 us
    pallas_call x3, Pallas kernels, transform(): out, place = call(place, basis, traces)  46.5 us
  transfers between devices with their start and end apart: 59, of which 23 were waited for; matrix products, arithmetic and copies ran while one was open for 2% of the time, Pallas kernels for 9%

profile of v2, /device:TPU:0, one launch (start us, length us, event | category | flops | bytes accessed | tf_op | source)
XLA Modules:
  0.0 1186.9 jit_solution(5491349293149474126)
XLA Ops:
  7.1 17.7 %shard_map.28 = (bf16[256,48,384]{2,1,0:T(8,128)(2,1)}, s32[1]{0:T(128)}) custom-call(s32[1]{0:T(128)} %bitcast.pos_ref, bf16[256,512]{1,0:T(8,128)(2,1)} %reshape.174.refs_0_, bf16[4,48,96,512]{3,2,1,0:T(8,128)(2,1)} %bitcast.77), custom_call_target="tpu_custom_call" | custom-call | tf_op jit(solution)/shard_map/pallas_call | solution.py:148
  24.8 14.4 %shard_map.29 = (bf16[128,48,384]{2,1,0:T(8,128)(2,1)}, s32[1]{0:T(128)}) custom-call(s32[1]{0:T(128)} %get-tuple-element.62.pos_ref, bf16[128,512]{1,0:T(8,128)(2,1)} %reshape.176.refs_0_, bf16[4,48,96,512]{3,2,1,0:T(8,128)(2,1)} %bitcast.78), custom_call_target="tpu_custom_call" | custom-call | tf_op jit(solution)/shard_map/pallas_call | solution.py:148
  39.2 14.4 %shard_map.30 = (bf16[128,48,384]{2,1,0:T(8,128)(2,1)}, s32[1]{0:T(128)}) custom-call(s32[1]{0:T(128)} %get-tuple-element.63.pos_ref, bf16[128,512]{1,0:T(8,128)(2,1)} %reshape.177.refs_0_, bf16[4,48,96,512]{3,2,1,0:T(8,128)(2,1)} %bitcast.79), custom_call_target="tpu_custom_call" | custom-call | tf_op jit(solution)/shard_map/pallas_call | solution.py:148
  53.6 60.0 %all_to_all.30 = bf16[8,4,2,2,48,384]{5,4,3,2,1,0:T(8,128)(2,1)} all-to-all(bf16[8,4,2,2,48,384]{5,4,3,2,1,0:T(8,128)(2,1)} %bitcast.87), channel_id=1, replica_groups=mesh['shot'=4,'rcv'=8] {'rcv'}, dimensions={0} | all-to-all | bytes 9437184 | tf_op jit(solution)/shard_map/all_to_all | solution.py:570
  126.9 25.4 %collective-permute-done.8 = bf16[8,2,2,48,384]{4,3,2,1,0:T(8,128)(2,1)S(1)} collective-permute-done((bf16[8,2,2,48,384]{4,3,2,1,0:T(8,128)(2,1)S(1)}, bf16[8,2,2,48,384]{4,3,2,1,0:T(8,128)(2,1)S(1)}, u32[]{:S(2)}, u32[]{:S(2)}) %collective-permute-start.8) | collective-permute-done | bytes 1179680 | tf_op jit(solution)/shard_map/ppermute | solution.py:544
  152.3 75.0 %collective-permute-done.7 = bf16[8,2,2,48,384]{4,3,2,1,0:T(8,128)(2,1)S(1)} collective-permute-done((bf16[8,2,2,48,384]{4,3,2,1,0:T(8,128)(2,1)S(1)}, bf16[8,2,2,48,384]{4,3,2,1,0:T(8,128)(2,1)S(1)}, u32[]{:S(2)}, u32[]{:S(2)}) %collective-permute-start.7) | collective-permute-done | bytes 1179680 | tf_op jit(solution)/shard_map/ppermute | solution.py:544
  253.6 27.5 %collective-permute-done.14.refs_11_ = bf16[1,2,2,2,48,384]{5,4,3,2,1,0:T(8,128)(2,1)S(1)} collective-permute-done((bf16[1,2,2,2,48,384]{5,4,3,2,1,0:T(8,128)(2,1)S(1)}, bf16[1,2,2,2,48,384]{5,4,3,2,1,0:T(8,128)(2,1)S(1)}, u32[]{:S(2)}, u32[]{:S(2)}) %collective-permute-start.14) | collective-permute-done | bytes 294944 | tf_op jit(solution)/shard_map/ppermute | solution.py:204
  301.5 10.8 collective-permute-start.9
  314.6 10.5 shard_map.31
  325.2 23.0 %shard_map.32 = (bf16[4,2,2,2,48,384]{5,4,3,2,1,0:T(8,128)(2,1)}, bf16[4,2,2,2,48,384]{5,4,3,2,1,0:T(8,128)(2,1)}, bf16[4,2,2,2,48,384]{5,4,3,2,1,0:T(8,128)(2,1...) custom-call(s32[1]{0:T(128)} %get-tuple-element.66.pos_ref, ...), custom_call_target="tpu_custom_call" | custom-call | tf_op jit(solution)/shard_map/pallas_call | solution.py:414
  379.3 25.8 %collective-permute-done.23.refs_2_.refs_3_ = bf16[3,2,2,2,48,384]{5,4,3,2,1,0:T(8,128)(2,1)} collective-permute-done((bf16[3,2,2,2,48,384]{5,4,3,2,1,0:T(8,128)(2,1)}, bf16[3,2,2,2,48,384]{5,4,3,2,1,0:T(8,128)(2,1)}, u32[]{:S(2)}, u32[]{:S(2)}) %collective-permute-start.23) | collective-permute-done | bytes 884768 | tf_op jit(solution)/shard_map/ppermute | solution.py:550
  416.3 51.5 %collective-permute-start.17 = (bf16[3,2,4,2,48,384]{5,4,3,2,1,0:T(8,128)(2,1)}, bf16[3,2,4,2,48,384]{5,4,3,2,1,0:T(8,128)(2,1)}, u32[]{:S(2)}, u32[]{:S(2)}) collective-permute-start(bf16[3,2,4,2,48,384]{5,4,3,2,1,0:T(8,128)(2,1)} %get-tuple-element.73), channel_id=1, source_target_pairs={{0,16},{8,24},{1,17},{9,25},{2,18},{10,26},{3,19},{11,27},{4,20},{... | collective-permute-start | bytes 5308424 | tf_op jit(solution)/shard_map/ppermute | solution.py:550
  470.4 104.8 %collective-permute-done.20.refs_7_ = bf16[2,2,4,2,48,384]{5,4,3,2,1,0:T(8,128)(2,1)} collective-permute-done((bf16[2,2,4,2,48,384]{5,4,3,2,1,0:T(8,128)(2,1)}, bf16[2,2,4,2,48,384]{5,4,3,2,1,0:T(8,128)(2,1)}, u32[]{:S(2)}, u32[]{:S(2)}) %collective-permute-start.20) | collective-permute-done | bytes 1179680 | tf_op jit(solution)/shard_map/ppermute | solution.py:550
  578.8 64.7 %collective-permute-done.18.refs_5_ = bf16[3,2,4,2,48,384]{5,4,3,2,1,0:T(8,128)(2,1)} collective-permute-done((bf16[3,2,4,2,48,384]{5,4,3,2,1,0:T(8,128)(2,1)}, bf16[3,2,4,2,48,384]{5,4,3,2,1,0:T(8,128)(2,1)}, u32[]{:S(2)}, u32[]{:S(2)}) %collective-permute-start.18) | collective-permute-done | bytes 1769504 | tf_op jit(solution)/shard_map/ppermute | solution.py:550
  649.9 54.8 %shard_map.34 = (bf16[4,2,4,2,48,384]{5,4,3,2,1,0:T(8,128)(2,1)}, bf16[4,2,4,2,48,384]{5,4,3,2,1,0:T(8,128)(2,1)}, bf16[4,2,4,2,48,384]{5,4,3,2,1,0:T(8,128)(2,1...) custom-call(s32[1]{0:T(128)} %get-tuple-element.70.pos_ref, ...), custom_call_target="tpu_custom_call" | custom-call | tf_op jit(solution)/shard_map/pallas_call | solution.py:414
  707.9 29.1 %shard_map.36 = (bf16[8,4,2,2,48,384]{5,4,3,2,1,0:T(8,128)(2,1)}, s32[1]{0:T(128)}) custom-call(s32[1]{0:T(128)} %get-tuple-element.82.pos_ref, f32[2,768,2]{2,1,0:T(8,128)} %get-tuple-element.139.refs_0_, bf16[4,2,4,2,2,48,384]{6,5,4,3,2,1,0:T(8,128)(2,1)} %bitcast.76, bf16[4,2,2,2,48,384]{5,4,3,2,1,0:T(8,128)(2,1)} %collective-permute-done.25.refs_2_, ...), custom_call_target="tpu_custom_call" | custom-call | tf_op jit(solution)/shard_map/pallas_call | solution.py:414
  776.6 10.7 collective-permute-done.37.refs_11_
  819.2 65.6 %collective-permute-done.41.refs_2_.refs_3_ = bf16[3,2,4,2,48,384]{5,4,3,2,1,0:T(8,128)(2,1)S(1)} collective-permute-done((bf16[3,2,4,2,48,384]{5,4,3,2,1,0:T(8,128)(2,1)}, bf16[3,2,4,2,48,384]{5,4,3,2,1,0:T(8,128)(2,1)S(1)}, u32[]{:S(2)}, u32[]{:S(2)}) %collective-permute-start.41) | collective-permute-done | bytes 1769504 | tf_op jit(solution)/shard_map/ppermute | solution.py:550
  887.1 11.1 collective-permute-done.42.refs_3_.refs_4_
  906.5 75.3 %collective-permute-start.46 = (bf16[1,2,4,2,48,384]{5,4,3,2,1,0:T(8,128)(2,1)}, bf16[1,2,4,2,48,384]{5,4,3,2,1,0:T(8,128)(2,1)S(1)}, u32[]{:S(2)}, u32[]{:S(2)}) collective-permute-start(bf16[1,2,4,2,48,384]{5,4,3,2,1,0:T(8,128)(2,1)} %get-tuple-element.109), channel_id=1, source_target_pairs={{0,8},{8,16},{16,24},{1,9},{9,17},{17,25},{2,10},{10,18},{18,26},{... | collective-permute-start | bytes 1769480 | tf_op jit(solution)/shard_map/ppermute | solution.py:593
  1008.5 23.8 %collective-permute-done.49.refs_11_ = bf16[1,2,4,2,48,384]{5,4,3,2,1,0:T(8,128)(2,1)} collective-permute-done((bf16[1,2,4,2,48,384]{5,4,3,2,1,0:T(8,128)(2,1)}, bf16[1,2,4,2,48,384]{5,4,3,2,1,0:T(8,128)(2,1)}, u32[]{:S(2)}, u32[]{:S(2)}) %collective-permute-start.49) | collective-permute-done | bytes 589856 | tf_op jit(solution)/shard_map/ppermute | solution.py:593
  1058.1 25.6 %collective-permute-done.53 = bf16[8,2,2,48,384]{4,3,2,1,0:T(8,128)(2,1)S(1)} collective-permute-done((bf16[8,2,2,48,384]{4,3,2,1,0:T(8,128)(2,1)}, bf16[8,2,2,48,384]{4,3,2,1,0:T(8,128)(2,1)S(1)}, u32[]{:S(2)}, u32[]{:S(2)}) %collective-permute-start.53) | collective-permute-done | bytes 1179680 | tf_op jit(solution)/shard_map/ppermute | solution.py:544
  1083.7 74.1 %collective-permute-done.52 = bf16[8,2,2,48,384]{4,3,2,1,0:T(8,128)(2,1)S(1)} collective-permute-done((bf16[8,2,2,48,384]{4,3,2,1,0:T(8,128)(2,1)}, bf16[8,2,2,48,384]{4,3,2,1,0:T(8,128)(2,1)S(1)}, u32[]{:S(2)}, u32[]{:S(2)}) %collective-permute-start.52) | collective-permute-done | bytes 1179680 | tf_op jit(solution)/shard_map/ppermute | solution.py:544
  1158.8 28.1 %shard_map.40 = (bf16[4,48,96,512]{3,2,1,0:T(8,128)(2,1)}, s32[1]{0:T(128)}) custom-call(s32[1]{0:T(128)} %get-tuple-element.114.pos_ref, bf16[512,512]{1,0:T(8,128)(2,1)} %copy-done.7, bf16[128,48,384]{2,1,0:T(8,128)(2,1)} %bitcast.30.refs_1_, bf16[256,48,384]{2,1,0:T(8,128)(2,1)} %bitcast.32.refs_2_, bf16[32,48,384]{2,1,0:T(8,128)(2,1)} %bitcast.84, ...), custom_call_target="tpu_custom_call" | custom-call | tf_op jit(solution)/shard_map/pallas_call | solution.py:192
  (202 shorter events, 262.3 us)
Async XLA Ops:
  113.6 116.2 %all-to-all-start = ((bf16[8,4,4,2,48,384]{5,4,3,2,1,0:T(8,128)(2,1)}), bf16[8,4,4,2,48,384]{5,4,3,2,1,0:T(8,128)(2,1)}, u32[]{:S(2)}, u32[]{:S(2)}) async-start(bf16[8,4,4,2,48,384]{5,4,3,2,1,0:T(8,128)(2,1)} %bitcast.83), calls=%async_computation | async-start | bytes 18874368 | tf_op jit(solution)/shard_map/all_to_all | solution.py:570
  125.9 101.4 %collective-permute-start.7 = (bf16[8,2,2,48,384]{4,3,2,1,0:T(8,128)(2,1)S(1)}, bf16[8,2,2,48,384]{4,3,2,1,0:T(8,128)(2,1)S(1)}, u32[]{:S(2)}, u32[]{:S(2)}) collective-permute-start(bf16[8,2,2,48,384]{4,3,2,1,0:T(8,128)(2,1)S(1)} %get-tuple-element.137), channel_id=1, source_target_pairs={{0,16},{8,24},{16,0},{24,8},{1,17},{9,25},{17,1},{25,9},{2,18},{10... | collective-permute-start | bytes 3538952 | tf_op jit(solution)/shard_map/ppermute | solution.py:544
  125.9 101.4 %collective-permute-start.6 = (bf16[8,2,2,48,384]{4,3,2,1,0:T(8,128)(2,1)S(1)}, bf16[8,2,2,48,384]{4,3,2,1,0:T(8,128)(2,1)S(1)}, u32[]{:S(2)}, u32[]{:S(2)}) collective-permute-start(bf16[8,2,2,48,384]{4,3,2,1,0:T(8,128)(2,1)S(1)} %get-tuple-element.138), channel_id=1, source_target_pairs={{0,8},{8,16},{16,24},{24,0},{1,9},{9,17},{17,25},{25,1},{2,10},{10... | collective-permute-start | bytes 3538952 | tf_op jit(solution)/shard_map/ppermute | solution.py:544
  229.8 95.3 %all-to-all-start.1 = ((bf16[8,4,2,2,48,384]{5,4,3,2,1,0:T(8,128)(2,1)}), bf16[8,4,2,2,48,384]{5,4,3,2,1,0:T(8,128)(2,1)}, u32[]{:S(2)}, u32[]{:S(2)}) async-start(bf16[8,4,2,2,48,384]{5,4,3,2,1,0:T(8,128)(2,1)} %pad_maximum_fusion), calls=%async_computation.1 | async-start | bytes 9437184 | tf_op jit(solution)/shard_map/all_to_all | solution.py:575
  359.9 107.9 %collective-permute-start.22 = (bf16[4,2,2,2,48,384]{5,4,3,2,1,0:T(8,128)(2,1)}, bf16[4,2,2,2,48,384]{5,4,3,2,1,0:T(8,128)(2,1)}, u32[]{:S(2)}, u32[]{:S(2)}) collective-permute-start(bf16[4,2,2,2,48,384]{5,4,3,2,1,0:T(8,128)(2,1)} %get-tuple-element.79), channel_id=1, source_target_pairs={{0,8},{8,16},{16,24},{1,9},{9,17},{17,25},{2,10},{10,18},{18,26},{... | collective-permute-start | bytes 3538952 | tf_op jit(solution)/shard_map/ppermute | solution.py:550
  377.0 92.0 %collective-permute-start.19 = (bf16[2,2,4,2,48,384]{5,4,3,2,1,0:T(8,128)(2,1)}, bf16[2,2,4,2,48,384]{5,4,3,2,1,0:T(8,128)(2,1)}, u32[]{:S(2)}, u32[]{:S(2)}) collective-permute-start(bf16[2,2,4,2,48,384]{5,4,3,2,1,0:T(8,128)(2,1)} %get-tuple-element.75), channel_id=1, source_target_pairs={{0,24},{1,25},{2,26},{3,27},{4,28},{5,29},{6,30},{7,31}} | collective-permute-start | bytes 3538952 | tf_op jit(solution)/shard_map/ppermute | solution.py:550
  405.1 240.7 %collective-permute-start.15 = (bf16[4,2,4,2,48,384]{5,4,3,2,1,0:T(8,128)(2,1)}, bf16[4,2,4,2,48,384]{5,4,3,2,1,0:T(8,128)(2,1)}, u32[]{:S(2)}, u32[]{:S(2)}) collective-permute-start(bf16[4,2,4,2,48,384]{5,4,3,2,1,0:T(8,128)(2,1)} %get-tuple-element.71), channel_id=1, source_target_pairs={{0,8},{8,16},{16,24},{1,9},{9,17},{17,25},{2,10},{10,18},{18,26},{... | collective-permute-start | bytes 7077896 | tf_op jit(solution)/shard_map/ppermute | solution.py:550
  415.0 232.1 %collective-permute-start.16 = (bf16[4,2,4,2,48,384]{5,4,3,2,1,0:T(8,128)(2,1)}, bf16[4,2,4,2,48,384]{5,4,3,2,1,0:T(8,128)(2,1)}, u32[]{:S(2)}, u32[]{:S(2)}) collective-permute-start(bf16[4,2,4,2,48,384]{5,4,3,2,1,0:T(8,128)(2,1)} %get-tuple-element.72), channel_id=1, source_target_pairs={{8,0},{16,8},{24,16},{9,1},{17,9},{25,17},{10,2},{18,10},{26,18},{... | collective-permute-start | bytes 7077896 | tf_op jit(solution)/shard_map/ppermute | solution.py:550
  416.3 161.2 %collective-permute-start.17 = (bf16[3,2,4,2,48,384]{5,4,3,2,1,0:T(8,128)(2,1)}, bf16[3,2,4,2,48,384]{5,4,3,2,1,0:T(8,128)(2,1)}, u32[]{:S(2)}, u32[]{:S(2)}) collective-permute-start(bf16[3,2,4,2,48,384]{5,4,3,2,1,0:T(8,128)(2,1)} %get-tuple-element.73), channel_id=1, source_target_pairs={{0,16},{8,24},{1,17},{9,25},{2,18},{10,26},{3,19},{11,27},{4,20},{... | collective-permute-start | bytes 5308424 | tf_op jit(solution)/shard_map/ppermute | solution.py:550
  467.8 175.7 %collective-permute-start.18 = (bf16[3,2,4,2,48,384]{5,4,3,2,1,0:T(8,128)(2,1)}, bf16[3,2,4,2,48,384]{5,4,3,2,1,0:T(8,128)(2,1)}, u32[]{:S(2)}, u32[]{:S(2)}) collective-permute-start(bf16[3,2,4,2,48,384]{5,4,3,2,1,0:T(8,128)(2,1)} %get-tuple-element.74), channel_id=1, source_target_pairs={{16,0},{24,8},{17,1},{25,9},{18,2},{26,10},{19,3},{27,11},{20,4},{... | collective-permute-start | bytes 5308424 | tf_op jit(solution)/shard_map/ppermute | solution.py:550
  469.1 106.1 %collective-permute-start.20 = (bf16[2,2,4,2,48,384]{5,4,3,2,1,0:T(8,128)(2,1)}, bf16[2,2,4,2,48,384]{5,4,3,2,1,0:T(8,128)(2,1)}, u32[]{:S(2)}, u32[]{:S(2)}) collective-permute-start(bf16[2,2,4,2,48,384]{5,4,3,2,1,0:T(8,128)(2,1)} %get-tuple-element.76), channel_id=1, source_target_pairs={{24,0},{25,1},{26,2},{27,3},{28,4},{29,5},{30,6},{31,7}} | collective-permute-start | bytes 3538952 | tf_op jit(solution)/shard_map/ppermute | solution.py:550
  575.1 132.8 %collective-permute-start.25 = (bf16[4,2,2,2,48,384]{5,4,3,2,1,0:T(8,128)(2,1)}, bf16[4,2,2,2,48,384]{5,4,3,2,1,0:T(8,128)(2,1)}, u32[]{:S(2)}, u32[]{:S(2)}) collective-permute-start(bf16[4,2,2,2,48,384]{5,4,3,2,1,0:T(8,128)(2,1)} %get-tuple-element.83), channel_id=1, source_target_pairs={{0,8},{8,16},{16,24},{1,9},{9,17},{17,25},{2,10},{10,18},{18,26},{... | collective-permute-start | bytes 3538952 | tf_op jit(solution)/shard_map/ppermute | solution.py:550
  577.5 130.4 %collective-permute-start.26 = (bf16[4,2,2,2,48,384]{5,4,3,2,1,0:T(8,128)(2,1)}, bf16[4,2,2,2,48,384]{5,4,3,2,1,0:T(8,128)(2,1)}, u32[]{:S(2)}, u32[]{:S(2)}) collective-permute-start(bf16[4,2,2,2,48,384]{5,4,3,2,1,0:T(8,128)(2,1)} %get-tuple-element.84), channel_id=1, source_target_pairs={{8,0},{16,8},{24,16},{9,1},{17,9},{25,17},{10,2},{18,10},{26,18},{... | collective-permute-start | bytes 3538952 | tf_op jit(solution)/shard_map/ppermute | solution.py:550
  796.5 245.7 %all-to-all-start.3 = ((bf16[8,4,2,2,48,384]{5,4,3,2,1,0:T(8,128)(2,1)}), bf16[8,4,2,2,48,384]{5,4,3,2,1,0:T(8,128)(2,1)}, u32[]{:S(2)}, u32[]{:S(2)}) async-start(bf16[8,4,2,2,48,384]{5,4,3,2,1,0:T(8,128)(2,1)} %bitcast.86), calls=%async_computation.3 | async-start | bytes 9437184 | tf_op jit(solution)/shard_map/all_to_all | solution.py:600
  802.4 95.8 %collective-permute-start.39 = (bf16[4,2,4,2,48,384]{5,4,3,2,1,0:T(8,128)(2,1)}, bf16[4,2,4,2,48,384]{5,4,3,2,1,0:T(8,128)(2,1)S(1)}, u32[]{:S(2)}, u32[]{:S(2)}) collective-permute-start(bf16[4,2,4,2,48,384]{5,4,3,2,1,0:T(8,128)(2,1)} %get-tuple-element.100), channel_id=1, source_target_pairs={{8,0},{16,8},{24,16},{9,1},{17,9},{25,17},{10,2},{18,10},{26,18},{... | collective-permute-start | bytes 7077896 | tf_op jit(solution)/shard_map/ppermute | solution.py:550
  803.7 94.5 %collective-permute-start.40 = (bf16[4,2,4,2,48,384]{5,4,3,2,1,0:T(8,128)(2,1)}, bf16[4,2,4,2,48,384]{5,4,3,2,1,0:T(8,128)(2,1)}, u32[]{:S(2)}, u32[]{:S(2)}) collective-permute-start(bf16[4,2,4,2,48,384]{5,4,3,2,1,0:T(8,128)(2,1)} %get-tuple-element.101), channel_id=1, source_target_pairs={{0,8},{8,16},{16,24},{1,9},{9,17},{17,25},{2,10},{10,18},{18,26},{... | collective-permute-start | bytes 7077896 | tf_op jit(solution)/shard_map/ppermute | solution.py:550
  809.8 88.4 %collective-permute-start.42 = (bf16[3,2,4,2,48,384]{5,4,3,2,1,0:T(8,128)(2,1)}, bf16[3,2,4,2,48,384]{5,4,3,2,1,0:T(8,128)(2,1)S(1)}, u32[]{:S(2)}, u32[]{:S(2)}) collective-permute-start(bf16[3,2,4,2,48,384]{5,4,3,2,1,0:T(8,128)(2,1)} %get-tuple-element.103), channel_id=1, source_target_pairs={{0,16},{8,24},{1,17},{9,25},{2,18},{10,26},{3,19},{11,27},{4,20},{... | collective-permute-start | bytes 5308424 | tf_op jit(solution)/shard_map/ppermute | solution.py:550
  817.9 165.5 %collective-permute-start.43 = (bf16[2,2,4,2,48,384]{5,4,3,2,1,0:T(8,128)(2,1)}, bf16[2,2,4,2,48,384]{5,4,3,2,1,0:T(8,128)(2,1)S(1)}, u32[]{:S(2)}, u32[]{:S(2)}) collective-permute-start(bf16[2,2,4,2,48,384]{5,4,3,2,1,0:T(8,128)(2,1)} %get-tuple-element.106), channel_id=1, source_target_pairs={{24,0},{25,1},{26,2},{27,3},{28,4},{29,5},{30,6},{31,7}} | collective-permute-start | bytes 3538952 | tf_op jit(solution)/shard_map/ppermute | solution.py:550
  884.8 103.2 %collective-permute-start.44 = (bf16[2,2,4,2,48,384]{5,4,3,2,1,0:T(8,128)(2,1)}, bf16[2,2,4,2,48,384]{5,4,3,2,1,0:T(8,128)(2,1)}, u32[]{:S(2)}, u32[]{:S(2)}) collective-permute-start(bf16[2,2,4,2,48,384]{5,4,3,2,1,0:T(8,128)(2,1)} %get-tuple-element.107), channel_id=1, source_target_pairs={{0,24},{1,25},{2,26},{3,27},{4,28},{5,29},{6,30},{7,31}} | collective-permute-start | bytes 3538952 | tf_op jit(solution)/shard_map/ppermute | solution.py:550
  905.2 89.1 %collective-permute-start.45 = (bf16[1,2,4,2,48,384]{5,4,3,2,1,0:T(8,128)(2,1)}, bf16[1,2,4,2,48,384]{5,4,3,2,1,0:T(8,128)(2,1)S(1)}, u32[]{:S(2)}, u32[]{:S(2)}) collective-permute-start(bf16[1,2,4,2,48,384]{5,4,3,2,1,0:T(8,128)(2,1)} %get-tuple-element.108), channel_id=1, source_target_pairs={{8,0},{16,8},{24,16},{9,1},{17,9},{25,17},{10,2},{18,10},{26,18},{... | collective-permute-start | bytes 1769480 | tf_op jit(solution)/shard_map/ppermute | solution.py:593
  906.5 91.6 %collective-permute-start.46 = (bf16[1,2,4,2,48,384]{5,4,3,2,1,0:T(8,128)(2,1)}, bf16[1,2,4,2,48,384]{5,4,3,2,1,0:T(8,128)(2,1)S(1)}, u32[]{:S(2)}, u32[]{:S(2)}) collective-permute-start(bf16[1,2,4,2,48,384]{5,4,3,2,1,0:T(8,128)(2,1)} %get-tuple-element.109), channel_id=1, source_target_pairs={{0,8},{8,16},{16,24},{1,9},{9,17},{17,25},{2,10},{10,18},{18,26},{... | collective-permute-start | bytes 1769480 | tf_op jit(solution)/shard_map/ppermute | solution.py:593
  1042.2 115.6 %all-to-all-start.4 = ((bf16[8,4,4,2,48,384]{5,4,3,2,1,0:T(8,128)(2,1)}), bf16[8,4,4,2,48,384]{5,4,3,2,1,0:T(8,128)(2,1)}, u32[]{:S(2)}, u32[]{:S(2)}) async-start(bf16[8,4,4,2,48,384]{5,4,3,2,1,0:T(8,128)(2,1)} %bitcast.82), calls=%async_computation.4 | async-start | bytes 18874368 | tf_op jit(solution)/shard_map/all_to_all | solution.py:600
  1056.9 100.9 %collective-permute-start.52 = (bf16[8,2,2,48,384]{4,3,2,1,0:T(8,128)(2,1)}, bf16[8,2,2,48,384]{4,3,2,1,0:T(8,128)(2,1)S(1)}, u32[]{:S(2)}, u32[]{:S(2)}) collective-permute-start(bf16[8,2,2,48,384]{4,3,2,1,0:T(8,128)(2,1)} %get-tuple-element.126), channel_id=1, source_target_pairs={{0,16},{8,24},{16,0},{24,8},{1,17},{9,25},{17,1},{25,9},{2,18},{10... | collective-permute-start | bytes 3538952 | tf_op jit(solution)/shard_map/ppermute | solution.py:544
  1056.9 100.9 %collective-permute-start.51 = (bf16[8,2,2,48,384]{4,3,2,1,0:T(8,128)(2,1)}, bf16[8,2,2,48,384]{4,3,2,1,0:T(8,128)(2,1)}, u32[]{:S(2)}, u32[]{:S(2)}) collective-permute-start(bf16[8,2,2,48,384]{4,3,2,1,0:T(8,128)(2,1)} %get-tuple-element.127), channel_id=1, source_target_pairs={{0,8},{8,16},{16,24},{24,0},{1,9},{9,17},{17,25},{25,1},{2,10},{10... | collective-permute-start | bytes 3538952 | tf_op jit(solution)/shard_map/ppermute | solution.py:544
  (67 other events, 2030.7 us)
